TPU v7x, 128 devices: a whole 4x4x4 slice. The times are simulated.
128 devices in a mesh: sub: 16 (over z, x), grp: 8 (over y, core).
Axes of the slice: x: 4, y: 4, z: 4, core: 2. Of those that a mesh axis runs over, the one named last changes fastest.
Arguments:
- rhs: float32 [8, 64, 256, 256], P('grp', 'sub')
- counts: int32 [8, 64], P('grp', 'sub'), may hold values from 64 to 256, as said below
- solve_panel: bfloat16 [8, 64, 512, 512], P('grp', 'sub'), as said below
- dirichlet_panel: bfloat16 [8, 64, 512, 512], P('grp', 'sub'), as said below
- coupling: float32 [8, 64, 32, 512], P('grp', 'sub'), may hold values from -0.25 to 0.25
- corner_map: int32 [8, 64, 32], P('grp', 'sub'), may hold values from 0 to 2047
- coarse_inverse: float32 [16, 2048, 2048], P('sub', 'grp'), as said below
Outputs:
- multipliers: float32 [8, 64, 256, 256], P('grp', 'sub')
- residual: float32 [8, 64, 256, 256], P('grp', 'sub')
Inputs may be any that keep to these rules, and one draw needn't show every extreme that they name: `counts`: some pair has all 256 unknowns constrained. `solve_panel`: each panel is symmetric positive definite. `dirichlet_panel`: each panel is symmetric positive definite. `coarse_inverse`: each slab's matrix is symmetric positive definite.
All inputs are finite; a program needn't handle non-finite values.
Results may differ from a plain program's by a relative error of at most 0.0003.
Values sent between devices are 32-bit elements; how exact they have to be, the bound alone decides.
A program may use at most 128 MiB of HBM per device.

v0:
```python
import jax
import jax.numpy as jnp
from jax import lax
from jax.sharding import PartitionSpec as P

ITERS = 3
HIGH = lax.Precision.HIGHEST


def passed_along(block, axis, distance):
    devices = range(lax.axis_size(axis))
    route = [(i - distance, i) for i in devices if i - distance in devices]
    return lax.ppermute(block, axis, route)


def spread_faces(values):
    previous = passed_along(values[:, -1:], "sub", 1)
    prior = jnp.concatenate([previous, values[:, :-1]], axis=1)
    return jnp.concatenate([-prior, values], axis=3)


def face_jump(result, live_mask):
    width = result.shape[3] // 2
    following = passed_along(result[:, :1, :, :width], "sub", -1)
    next_left = jnp.concatenate([result[:, 1:, :, :width], following], axis=1)
    return live_mask * (result[..., width:] - next_left)


def panel_apply(panel, face_vals):
    return jnp.einsum(
        "gsrp,gsqp->gsrq", face_vals, panel, precision=HIGH, preferred_element_type=jnp.float32
    )


def inner(first, second):
    return jnp.sum(first * second, axis=(0, 1, 3))


def expand(scalars):
    return scalars[None, None, :, None]


def residual_sum(resid, precond):
    return lax.psum(inner(resid, precond), ("sub", "grp"))


def local(rhs, counts, solve_panel, dirichlet_panel, coupling, corner_map, coarse_inverse):
    local_subs = rhs.shape[1]
    width = rhs.shape[3]
    size = coarse_inverse.shape[2]
    last_device = lax.axis_index("sub") == lax.axis_size("sub") - 1
    slots = jnp.arange(local_subs, dtype=jnp.int32)
    positions = jnp.arange(width, dtype=jnp.int32)
    not_last = jnp.logical_not(last_device & (slots == local_subs - 1))
    live = (positions[None, None, :] < counts[:, :, None]) & not_last[None, :, None]
    live_mask = live.astype(jnp.float32)[:, :, None, :]
    corner_onehot = (corner_map[0][..., None] == jnp.arange(size, dtype=jnp.int32)).astype(
        jnp.float32
    )

    def precondition(values):
        return 0.25 * face_jump(panel_apply(dirichlet_panel, spread_faces(values)), live_mask)

    multipliers = jnp.zeros_like(rhs)
    residual = live_mask * rhs
    precond = precondition(residual)
    direction = precond
    rz_now = residual_sum(residual, precond)
    for step in range(ITERS):
        apply_face_vals = spread_faces(direction)
        corner_vals = jnp.einsum("srp,skp->srk", apply_face_vals[0], coupling[0], precision=HIGH)
        owned_totals = lax.psum_scatter(
            jnp.einsum("skn,srk->nr", corner_onehot, corner_vals, precision=HIGH),
            "grp",
            scatter_dimension=0,
            tiled=True,
        )
        partial_solved = jnp.einsum("mn,mr->nr", coarse_inverse[0], owned_totals, precision=HIGH)
        solved = lax.psum(partial_solved, "grp")
        back = jnp.einsum("skn,nr->srk", corner_onehot, solved, precision=HIGH)
        result = (
            panel_apply(solve_panel, apply_face_vals)
            + jnp.einsum("srk,skp->srp", back, coupling[0], precision=HIGH)[None]
        )
        image = face_jump(result, live_mask)
        alpha = rz_now / lax.psum(inner(direction, image), ("sub", "grp"))
        multipliers = multipliers + expand(alpha) * direction
        residual = residual - expand(alpha) * image
        if step + 1 < ITERS:
            precond = precondition(residual)
            rz_next = residual_sum(residual, precond)
            direction = precond + expand(rz_next / rz_now) * direction
            rz_now = rz_next
    return (multipliers, residual)


def solution(mesh):
    return jax.shard_map(
        local,
        mesh=mesh,
        in_specs=(
            P("grp", "sub", None, None),
            P("grp", "sub"),
            P("grp", "sub", None, None),
            P("grp", "sub", None, None),
            P("grp", "sub", None, None),
            P("grp", "sub", None),
            P("sub", "grp", None),
        ),
        out_specs=(P("grp", "sub", None, None), P("grp", "sub", None, None)),
        check_vma=False,
    )
```

profile of v0, /device:TPU:1, one launch (start us, length us, event | category | flops | bytes accessed | tf_op | source)
XLA Modules:
  0.0 832.8 jit_solution(642383770802080915)
XLA Ops:
  9.4 4.0 collective-permute-start
  13.5 4.9 collective-permute-done
  21.7 7.8 collective-permute-done.1
  29.7 3.2 collective-permute-start.2
  33.1 3.2 collective-permute-done.2
  36.4 1.9 fusion.29
  38.3 3.7 convolution_bitcast_fusion.2
  42.0 38.6 %reduce-scatter.4.cloned.1.call-done = f32[256,256]{1,0:T(8,128)} async-done(((f32[2048,256]{1,0:T(8,128)}), f32[256,256]{1,0:T(8,128)}) %reduce-scatter.4.cloned.1.call-update) | async-done | bytes 262160 | tf_op jit(solution)/shard_map/reduce_scatter | solution.py:72
  80.6 4.9 convolution_bitcast_fusion.5
  85.8 65.4 %all-reduce.5.cloned.1.call-done = f32[2048,256]{0,1:T(8,128)} async-done(((f32[2048,256]{0,1:T(8,128)}), f32[2048,256]{0,1:T(8,128)}) %all-reduce.5.cloned.1.call-update) | async-done | bytes 2097168 | tf_op jit(solution)/shard_map/psum | solution.py:79
  151.2 3.1 fusion.45
  154.3 1.8 fusion.78
  159.7 5.7 collective-permute-done.3
  166.2 70.6 %all-reduce = (f32[256]{0:T(256)S(1)}, f32[256]{0:T(256)S(1)}) all-reduce(f32[256]{0:T(256)S(1)} %get-tuple-element.3, f32[256]{0:T(256)S(1)} %get-tuple-element.2), channel_id=1, replica_groups=mesh['sub'=16,'grp'=8] {'sub','grp'}, use_global_device_ids=true, to_apply=%region_1.0 | all-reduce | flops 512 | bytes 4096 | tf_op jit(solution)/shard_map/psum | solution.py:44
  236.8 2.1 multiply_subtract_fusion.2
  238.9 2.5 collective-permute-start.4
  241.4 4.6 collective-permute-done.4
  249.4 7.5 collective-permute-done.5
  258.0 67.7 %psum.66 = f32[256]{0:T(256)S(1)} all-reduce(f32[256]{0:T(256)S(1)} %multiply_reduce_fusion.3), channel_id=1, replica_groups=mesh['sub'=16,'grp'=8] {'sub','grp'}, use_global_device_ids=true, to_apply=%region_7.0 | all-reduce | flops 256 | bytes 2048 | tf_op jit(solution)/shard_map/psum | solution.py:44
  325.7 2.1 multiply_add_fusion.2
  327.8 2.6 collective-permute-start.6
  330.5 4.6 collective-permute-done.6
  336.1 1.9 fusion.28
  338.0 3.7 convolution_bitcast_fusion.1
  341.7 32.0 %reduce-scatter.6.cloned.1.call-done = f32[256,256]{1,0:T(8,128)} async-done(((f32[2048,256]{1,0:T(8,128)}), f32[256,256]{1,0:T(8,128)}) %reduce-scatter.6.cloned.1.call-update) | async-done | bytes 262160 | tf_op jit(solution)/shard_map/reduce_scatter | solution.py:72
  373.7 4.9 convolution_bitcast_fusion.4
  378.7 65.6 %all-reduce.7.cloned.1.call-done = f32[2048,256]{0,1:T(8,128)} async-done(((f32[2048,256]{0,1:T(8,128)}), f32[2048,256]{0,1:T(8,128)}) %all-reduce.7.cloned.1.call-update) | async-done | bytes 2097168 | tf_op jit(solution)/shard_map/psum | solution.py:79
  444.4 3.1 fusion.48
  447.5 1.8 fusion.75
  452.6 5.7 collective-permute-done.7
  459.4 71.1 %psum.68 = f32[256]{0:T(256)S(1)} all-reduce(f32[256]{0:T(256)S(1)} %multiply_reduce_fusion.2), channel_id=1, replica_groups=mesh['sub'=16,'grp'=8] {'sub','grp'}, use_global_device_ids=true, to_apply=%region_11.0 | all-reduce | flops 256 | bytes 2048 | tf_op jit(solution)/shard_map/psum | solution.py:86
  530.5 2.1 multiply_subtract_fusion.1
  532.6 2.5 collective-permute-start.8
  535.1 4.6 collective-permute-done.8
  543.0 7.5 collective-permute-done.9
  551.6 67.7 %psum.69 = f32[256]{0:T(256)S(1)} all-reduce(f32[256]{0:T(256)S(1)} %multiply_reduce_fusion.1), channel_id=1, replica_groups=mesh['sub'=16,'grp'=8] {'sub','grp'}, use_global_device_ids=true, to_apply=%region_13.0 | all-reduce | flops 256 | bytes 2048 | tf_op jit(solution)/shard_map/psum | solution.py:44
  621.1 2.4 collective-permute-start.10
  623.6 4.8 collective-permute-done.10
  628.4 1.9 fusion.27
  630.3 3.7 convolution_bitcast_fusion
  634.3 31.8 %reduce-scatter.8.cloned.1.call-done = f32[256,256]{1,0:T(8,128)} async-done(((f32[2048,256]{1,0:T(8,128)}), f32[256,256]{1,0:T(8,128)}) %reduce-scatter.8.cloned.1.call-update) | async-done | bytes 262160 | tf_op jit(solution)/shard_map/reduce_scatter | solution.py:72
  666.1 4.9 convolution_bitcast_fusion.3
  671.0 65.7 %all-reduce.9.cloned.1.call-done = f32[2048,256]{0,1:T(8,128)} async-done(((f32[2048,256]{0,1:T(8,128)}), f32[2048,256]{0,1:T(8,128)}) %all-reduce.9.cloned.1.call-update) | async-done | bytes 2097168 | tf_op jit(solution)/shard_map/psum | solution.py:79
  736.7 3.1 fusion.51
  739.8 1.8 fusion.72
  744.9 5.7 collective-permute-done.11
  750.9 70.7 %psum.71 = f32[256]{0:T(256)S(1)} all-reduce(f32[256]{0:T(256)S(1)} %multiply_reduce_fusion), channel_id=1, replica_groups=mesh['sub'=16,'grp'=8] {'sub','grp'}, use_global_device_ids=true, to_apply=%region_17.0 | all-reduce | flops 256 | bytes 2048 | tf_op jit(solution)/shard_map/psum | solution.py:86
  821.6 4.1 multiply_subtract_fusion
  (137 shorter events, 30.4 us)
Async XLA Ops:
  7.2 11.3 %copy-start = (bf16[1,4,512,512]{3,2,1,0:T(8,128)(2,1)S(1)}, bf16[1,4,512,512]{3,2,1,0:T(8,128)(2,1)}, u32[]{:S(2)}) copy-start(bf16[1,4,512,512]{3,2,1,0:T(8,128)(2,1)} %param.10) | copy-start | bytes 6291460
  7.2 73.4 %reduce-scatter.4.cloned.1.call-start = ((), (), s32[]{:S(2)}) async-start(), calls=%async_computation.3 | async-start | bytes 2359296 | tf_op jit(solution)/shard_map/reduce_scatter | solution.py:72
  9.4 8.9 %collective-permute-start = (f32[1,1,256,256]{3,2,1,0:T(8,128)S(1)}, f32[1,1,256,256]{3,2,1,0:T(8,128)S(1)}, u32[]{:S(2)}, u32[]{:S(2)}) collective-permute-start(f32[1,1,256,256]{3,2,1,0:T(8,128)S(1)} %slice.120), channel_id=1, source_target_pairs={{0,8},{8,16},{16,24},{24,32},{32,40},{40,48},{48,56},{56,64},{64,7... | collective-permute-start | bytes 786440 | tf_op jit(solution)/shard_map/ppermute | solution.py:13
  20.3 9.2 %collective-permute-start.1 = (f32[1,1,256,256]{3,2,1,0:T(8,128)S(1)}, f32[1,1,256,256]{3,2,1,0:T(8,128)S(1)}, u32[]{:S(2)}, u32[]{:S(2)}) collective-permute-start(f32[1,1,256,256]{3,2,1,0:T(8,128)S(1)} %slice.124), channel_id=1, source_target_pairs={{8,0},{16,8},{24,16},{32,24},{40,32},{48,40},{56,48},{64,56},{72,6... | collective-permute-start | bytes 786440 | tf_op jit(solution)/shard_map/ppermute | solution.py:13
  29.7 6.7 copy-start.9
  29.7 135.8 %copy-start.8 = (f32[1,4,256,256]{3,2,1,0:T(8,128)}, f32[1,4,256,256]{3,2,1,0:T(8,128)S(1)}, u32[]{:S(2)}) copy-start(f32[1,4,256,256]{3,2,1,0:T(8,128)S(1)} %get-tuple-element.9) | copy-start | bytes 3145732
  29.7 6.6 copy-start.17
  29.7 6.5 collective-permute-start.2
  33.0 5.2 copy-start.33
  36.4 1.9 copy-start.18
  42.0 109.2 %all-reduce.5.cloned.1.call-start = ((), (), s32[]{:S(2)}) async-start(), calls=%async_computation.4 | async-start | bytes 4194304 | tf_op jit(solution)/shard_map/psum | solution.py:79
  85.5 288.2 %reduce-scatter.6.cloned.1.call-start = ((), (), s32[]{:S(2)}) async-start(), calls=%async_computation.5 | async-start | bytes 2359296 | tf_op jit(solution)/shard_map/reduce_scatter | solution.py:72
  151.2 5.0 copy-start.5
  151.2 5.0 copy-start.10
  151.2 5.0 copy-start.19
  158.0 7.9 copy-start.14
  158.0 7.4 copy-start.16
  158.1 7.4 collective-permute-start.3
  159.7 6.3 copy-start.25
  238.9 18.0 %copy-start.4 = (f32[1,4,256,256]{3,2,1,0:T(8,128)}, f32[1,4,256,256]{3,2,1,0:T(8,128)S(1)}, u32[]{:S(2)}) copy-start(f32[1,4,256,256]{3,2,1,0:T(8,128)S(1)} %multiply_subtract_fusion.2) | copy-start | bytes 3145732
  238.9 7.1 collective-permute-start.4
  248.0 8.9 %copy-start.11 = (f32[1,4,256,512]{3,2,1,0:T(8,128)}, f32[1,4,256,512]{3,2,1,0:T(8,128)S(1)}, u32[]{:S(2)}) copy-start(f32[1,4,256,512]{3,2,1,0:T(8,128)S(1)} %fusion.39) | copy-start | bytes 6291460
  248.0 8.9 %collective-permute-start.5 = (f32[1,1,256,256]{3,2,1,0:T(8,128)S(1)}, f32[1,1,256,256]{3,2,1,0:T(8,128)S(1)}, u32[]{:S(2)}, u32[]{:S(2)}) collective-permute-start(f32[1,1,256,256]{3,2,1,0:T(8,128)S(1)} %slice.134), channel_id=1, source_target_pairs={{8,0},{16,8},{24,16},{32,24},{40,32},{48,40},{56,48},{64,56},{72,6... | collective-permute-start | bytes 786440 | tf_op jit(solution)/shard_map/ppermute | solution.py:13
  249.4 7.5 copy-start.27
  327.8 7.2 collective-permute-start.6
  335.1 1.0 copy-start.20
  341.7 102.7 %all-reduce.7.cloned.1.call-start = ((), (), s32[]{:S(2)}) async-start(), calls=%async_computation.6 | async-start | bytes 4194304 | tf_op jit(solution)/shard_map/psum | solution.py:79
  378.7 287.4 %reduce-scatter.8.cloned.1.call-start = ((), (), s32[]{:S(2)}) async-start(), calls=%async_computation.7 | async-start | bytes 2359296 | tf_op jit(solution)/shard_map/reduce_scatter | solution.py:72
  444.4 5.0 copy-start.6
  444.4 5.0 copy-start.21
  451.2 7.2 copy-start.15
  451.2 7.1 collective-permute-start.7
  452.6 5.7 copy-start.26
  532.5 18.0 %copy-start.3 = (f32[1,4,256,256]{3,2,1,0:T(8,128)}, f32[1,4,256,256]{3,2,1,0:T(8,128)S(1)}, u32[]{:S(2)}) copy-start(f32[1,4,256,256]{3,2,1,0:T(8,128)S(1)} %multiply_subtract_fusion.1) | copy-start | bytes 3145732
  532.6 7.1 collective-permute-start.8
  541.6 8.9 %copy-start.12 = (f32[1,4,256,512]{3,2,1,0:T(8,128)}, f32[1,4,256,512]{3,2,1,0:T(8,128)S(1)}, u32[]{:S(2)}) copy-start(f32[1,4,256,512]{3,2,1,0:T(8,128)S(1)} %fusion.36) | copy-start | bytes 6291460
  541.6 8.9 %collective-permute-start.9 = (f32[1,1,256,256]{3,2,1,0:T(8,128)S(1)}, f32[1,1,256,256]{3,2,1,0:T(8,128)S(1)}, u32[]{:S(2)}, u32[]{:S(2)}) collective-permute-start(f32[1,1,256,256]{3,2,1,0:T(8,128)S(1)} %slice.144), channel_id=1, source_target_pairs={{8,0},{16,8},{24,16},{32,24},{40,32},{48,40},{56,48},{64,56},{72,6... | collective-permute-start | bytes 786440 | tf_op jit(solution)/shard_map/ppermute | solution.py:13
  543.0 7.5 copy-start.28
  621.1 7.4 copy-start.1
  621.1 7.2 collective-permute-start.10
  628.4 1.9 copy-start.22
  634.1 102.6 %all-reduce.9.cloned.1.call-start = ((), (), s32[]{:S(2)}) async-start(), calls=%async_computation.8 | async-start | bytes 4194304 | tf_op jit(solution)/shard_map/psum | solution.py:79
  736.7 5.0 copy-start.2
  736.7 5.0 copy-start.7
  736.7 5.0 copy-start.23
  743.5 7.2 copy-start.13
  743.6 7.1 collective-permute-start.11
  744.9 5.7 copy-start.24
  (4 other events, 2.8 us)
Sparse Core Ops, SparseCore 0:
  42.1 38.4 reduce-scatter.3
  85.7 65.4 all-reduce.4
  341.8 31.8 reduce-scatter.5
  378.8 65.5 all-reduce.6
  634.2 31.8 reduce-scatter.7
  671.1 65.4 all-reduce.8
where the time goes:
time: 841 us; the launch traced here: 833 us
  waiting for transfers between devices  366 us (44%)
  blocking collectives  348 us (41%)
  matrix products  57.2 us (7%)
  starting transfers between devices  25.7 us (3%)
  other arithmetic  16.7 us (2%)
  between operations  15.2 us (2%)
    psum x3, blocking collectives, residual_sum(): return lax.psum(inner(resid, precond), ('sub', 'grp'))  206 us
    psum x3, waiting for transfers between devices, local(): solved = lax.psum(partial_solved, 'grp')  197 us
    psum x2, blocking collectives, local(): alpha = rz_now / lax.psum(inner(direction, image), ('sub', 'grp'))  142 us
    reduce_scatter x3, waiting for transfers between devices, local(): lax.psum_scatter(jnp.einsum('skn,srk->nr', corner_onehot, corner_vals, pr...  102 us
    ppermute x12, waiting for transfers between devices, passed_along(): return lax.ppermute(block, axis, route)  66.6 us
    ppermute x12, starting transfers between devices, passed_along(): return lax.ppermute(block, axis, route)  25.1 us
  transfers between devices with their start and end apart: 18, of which 18 were waited for; matrix products, arithmetic and copies ran while one was open for 0% of the time, Pallas kernels for 0%

commit v1 on v0

--- a/solution.py
+++ b/solution.py
@@ -5,6 +5,15 @@
 
 ITERS = 3
 HIGH = lax.Precision.HIGHEST
+
+
+def doubling_sum(value, axis):
+    devices = lax.axis_size(axis)
+    total, hop = (value, 1)
+    while hop < devices:
+        total = total + lax.ppermute(total, axis, [(i, i ^ hop) for i in range(devices)])
+        hop = 2 * hop
+    return total
 
 
 def passed_along(block, axis, distance):
@@ -76,7 +85,7 @@
             tiled=True,
         )
         partial_solved = jnp.einsum("mn,mr->nr", coarse_inverse[0], owned_totals, precision=HIGH)
-        solved = lax.psum(partial_solved, "grp")
+        solved = doubling_sum(partial_solved, "grp")
         back = jnp.einsum("skn,nr->srk", corner_onehot, solved, precision=HIGH)
         result = (
             panel_apply(solve_panel, apply_face_vals)

time: 841 us -> 936 us (1.11)
  waiting for transfers between devices: 366 us -> 463 us
  starting transfers between devices: 25.7 us -> 39.3 us
  blocking collectives: 348 us -> 338 us
    ppermute x0 -> x9, waiting for transfers between devices: none -> 293 us  [doubling_sum(): lax.ppermute(total, axis, [(i, i ^ hop) for i in range(devices)])]
    psum x3 -> x0, waiting for transfers between devices: 197 us -> none  [local(): solved = lax.psum(partial_solved, 'grp')]
    ppermute x0 -> x9, starting transfers between devices: none -> 13.6 us  [doubling_sum(): lax.ppermute(total, axis, [(i, i ^ hop) for i in range(devices)])]
  transfers between devices with their start and end apart: 18 -> 24, of which waited for: 18 -> 24; matrix products, arithmetic and copies ran while one was open for 0% -> 0% of each run, Pallas kernels for 0% -> 0%
where the time goes in v1:
time: 936 us; the launch traced here: 927 us
  waiting for transfers between devices  463 us (49%)
  blocking collectives  338 us (36%)
  matrix products  48.2 us (5%)
  starting transfers between devices  39.3 us (4%)
  other arithmetic  18.6 us (2%)
  between operations  14.9 us (2%)
    ppermute x9, waiting for transfers between devices, doubling_sum(): lax.ppermute(total, axis, [(i, i ^ hop) for i in range(devices)])  293 us
    psum x3, blocking collectives, residual_sum(): return lax.psum(inner(resid, precond), ('sub', 'grp'))  202 us
    psum x2, blocking collectives, local(): alpha = rz_now / lax.psum(inner(direction, image), ('sub', 'grp'))  136 us
    reduce_scatter x3, waiting for transfers between devices, local(): lax.psum_scatter(jnp.einsum('skn,srk->nr', corner_onehot, corner_vals, pr...  102 us
    ppermute x12, waiting for transfers between devices, passed_along(): return lax.ppermute(block, axis, route)  68.3 us
    ppermute x12, starting transfers between devices, passed_along(): return lax.ppermute(block, axis, route)  25.5 us
  transfers between devices with their start and end apart: 24, of which 24 were waited for; matrix products, arithmetic and copies ran while one was open for 0% of the time, Pallas kernels for 0%

profile of v1, /device:TPU:1, one launch (start us, length us, event | category | flops | bytes accessed | tf_op | source)
XLA Modules:
  0.0 926.9 jit_solution(7916336470234231459)
XLA Ops:
  9.4 4.0 collective-permute-start
  13.5 4.9 collective-permute-done
  21.7 7.8 collective-permute-done.1
  29.7 3.2 collective-permute-start.2
  33.1 3.2 collective-permute-done.2
  38.3 3.7 convolution_bitcast_fusion.2
  42.0 38.6 %reduce-scatter.4.cloned.1.call-done = f32[256,256]{1,0:T(8,128)} async-done(((f32[2048,256]{1,0:T(8,128)}), f32[256,256]{1,0:T(8,128)}) %reduce-scatter.4.cloned.1.call-update) | async-done | bytes 262160 | tf_op jit(solution)/shard_map/reduce_scatter | solution.py:81
  80.6 3.6 convolution_bitcast_fusion.5
  84.2 3.7 collective-permute-start.3
  87.9 3.8 collective-permute-done.3
  92.1 46.8 %collective-permute-done.4 = f32[2048,256]{0,1:T(8,128)S(1)} collective-permute-done((f32[2048,256]{0,1:T(8,128)S(1)}, f32[2048,256]{0,1:T(8,128)S(1)}, u32[]{:S(2)}, u32[]{:S(2)}) %collective-permute-start.4) | collective-permute-done | bytes 2097184 | tf_op jit(solution)/shard_map/ppermute | solution.py:14
  139.9 46.9 %collective-permute-done.5 = f32[2048,256]{0,1:T(8,128)S(1)} collective-permute-done((f32[2048,256]{0,1:T(8,128)S(1)}, f32[2048,256]{0,1:T(8,128)S(1)}, u32[]{:S(2)}, u32[]{:S(2)}) %collective-permute-start.5) | collective-permute-done | bytes 2097184 | tf_op jit(solution)/shard_map/ppermute | solution.py:14
  193.8 6.2 collective-permute-done.6
  200.7 67.7 %all-reduce = (f32[256]{0:T(256)S(1)}, f32[256]{0:T(256)S(1)}) all-reduce(f32[256]{0:T(256)S(1)} %get-tuple-element.3, f32[256]{0:T(256)S(1)} %get-tuple-element.2), channel_id=1, replica_groups=mesh['sub'=16,'grp'=8] {'sub','grp'}, use_global_device_ids=true, to_apply=%region_1.0 | all-reduce | flops 512 | bytes 4096 | tf_op jit(solution)/shard_map/psum | solution.py:53
  268.4 2.1 multiply_subtract_fusion.2
  270.6 2.6 collective-permute-start.7
  273.3 4.7 collective-permute-done.7
  281.4 7.6 collective-permute-done.8
  290.1 67.3 %psum.44 = f32[256]{0:T(256)S(1)} all-reduce(f32[256]{0:T(256)S(1)} %multiply_reduce_fusion.3), channel_id=1, replica_groups=mesh['sub'=16,'grp'=8] {'sub','grp'}, use_global_device_ids=true, to_apply=%region_6.0 | all-reduce | flops 256 | bytes 2048 | tf_op jit(solution)/shard_map/psum | solution.py:53
  357.4 2.1 multiply_add_fusion.2
  359.5 2.6 collective-permute-start.9
  362.1 4.5 collective-permute-done.9
  369.6 3.7 convolution_bitcast_fusion.1
  373.3 31.8 %reduce-scatter.6.cloned.1.call-done = f32[256,256]{1,0:T(8,128)} async-done(((f32[2048,256]{1,0:T(8,128)}), f32[256,256]{1,0:T(8,128)}) %reduce-scatter.6.cloned.1.call-update) | async-done | bytes 262160 | tf_op jit(solution)/shard_map/reduce_scatter | solution.py:81
  405.2 3.6 convolution_bitcast_fusion.4
  408.8 3.7 collective-permute-start.10
  412.4 3.8 collective-permute-done.10
  416.7 46.8 %collective-permute-done.11 = f32[2048,256]{0,1:T(8,128)S(1)} collective-permute-done((f32[2048,256]{0,1:T(8,128)S(1)}, f32[2048,256]{0,1:T(8,128)S(1)}, u32[]{:S(2)}, u32[]{:S(2)}) %collective-permute-start.11) | collective-permute-done | bytes 2097184 | tf_op jit(solution)/shard_map/ppermute | solution.py:14
  464.8 46.9 %collective-permute-done.12 = f32[2048,256]{0,1:T(8,128)S(1)} collective-permute-done((f32[2048,256]{0,1:T(8,128)S(1)}, f32[2048,256]{0,1:T(8,128)S(1)}, u32[]{:S(2)}, u32[]{:S(2)}) %collective-permute-start.12) | collective-permute-done | bytes 2097184 | tf_op jit(solution)/shard_map/ppermute | solution.py:14
  518.3 6.2 collective-permute-done.13
  525.6 67.9 %psum.45 = f32[256]{0:T(256)S(1)} all-reduce(f32[256]{0:T(256)S(1)} %multiply_reduce_fusion.2), channel_id=1, replica_groups=mesh['sub'=16,'grp'=8] {'sub','grp'}, use_global_device_ids=true, to_apply=%region_9.0 | all-reduce | flops 256 | bytes 2048 | tf_op jit(solution)/shard_map/psum | solution.py:95
  593.5 2.1 multiply_subtract_fusion.1
  595.6 2.6 collective-permute-start.14
  598.3 4.8 collective-permute-done.14
  606.4 7.7 collective-permute-done.15
  615.1 67.2 %psum.46 = f32[256]{0:T(256)S(1)} all-reduce(f32[256]{0:T(256)S(1)} %multiply_reduce_fusion.1), channel_id=1, replica_groups=mesh['sub'=16,'grp'=8] {'sub','grp'}, use_global_device_ids=true, to_apply=%region_11.0 | all-reduce | flops 256 | bytes 2048 | tf_op jit(solution)/shard_map/psum | solution.py:53
  684.1 2.5 collective-permute-start.16
  686.7 4.6 collective-permute-done.16
  693.3 3.7 convolution_bitcast_fusion
  697.0 32.0 %reduce-scatter.8.cloned.1.call-done = f32[256,256]{1,0:T(8,128)} async-done(((f32[2048,256]{1,0:T(8,128)}), f32[256,256]{1,0:T(8,128)}) %reduce-scatter.8.cloned.1.call-update) | async-done | bytes 262160 | tf_op jit(solution)/shard_map/reduce_scatter | solution.py:81
  729.0 3.6 convolution_bitcast_fusion.3
  732.6 3.7 collective-permute-start.17
  736.3 3.8 collective-permute-done.17
  740.5 46.8 %collective-permute-done.18 = f32[2048,256]{0,1:T(8,128)S(1)} collective-permute-done((f32[2048,256]{0,1:T(8,128)S(1)}, f32[2048,256]{0,1:T(8,128)S(1)}, u32[]{:S(2)}, u32[]{:S(2)}) %collective-permute-start.18) | collective-permute-done | bytes 2097184 | tf_op jit(solution)/shard_map/ppermute | solution.py:14
  788.3 46.9 %collective-permute-done.19 = f32[2048,256]{0,1:T(8,128)S(1)} collective-permute-done((f32[2048,256]{0,1:T(8,128)S(1)}, f32[2048,256]{0,1:T(8,128)S(1)}, u32[]{:S(2)}, u32[]{:S(2)}) %collective-permute-start.19) | collective-permute-done | bytes 2097184 | tf_op jit(solution)/shard_map/ppermute | solution.py:14
  841.8 6.2 collective-permute-done.20
  848.2 67.8 %psum.47 = f32[256]{0:T(256)S(1)} all-reduce(f32[256]{0:T(256)S(1)} %multiply_reduce_fusion), channel_id=1, replica_groups=mesh['sub'=16,'grp'=8] {'sub','grp'}, use_global_device_ids=true, to_apply=%region_14.0 | all-reduce | flops 256 | bytes 2048 | tf_op jit(solution)/shard_map/psum | solution.py:95
  916.1 4.1 multiply_subtract_fusion
  (152 shorter events, 49.8 us)
Async XLA Ops:
  7.2 11.3 %copy-start = (bf16[1,4,512,512]{3,2,1,0:T(8,128)(2,1)S(1)}, bf16[1,4,512,512]{3,2,1,0:T(8,128)(2,1)}, u32[]{:S(2)}) copy-start(bf16[1,4,512,512]{3,2,1,0:T(8,128)(2,1)} %param.10) | copy-start | bytes 6291460
  7.2 73.4 %reduce-scatter.4.cloned.1.call-start = ((), (), s32[]{:S(2)}) async-start(), calls=%async_computation.3 | async-start | bytes 2359296 | tf_op jit(solution)/shard_map/reduce_scatter | solution.py:81
  9.4 8.9 collective-permute-start
  20.3 9.2 collective-permute-start.1
  29.7 6.7 copy-start.9
  29.7 170.3 %copy-start.8 = (f32[1,4,256,256]{3,2,1,0:T(8,128)}, f32[1,4,256,256]{3,2,1,0:T(8,128)S(1)}, u32[]{:S(2)}) copy-start(f32[1,4,256,256]{3,2,1,0:T(8,128)S(1)} %get-tuple-element.9) | copy-start | bytes 3145732
  29.7 6.6 copy-start.17
  29.7 6.5 collective-permute-start.2
  33.0 5.2 copy-start.33
  36.4 1.9 copy-start.18
  42.0 363.2 %reduce-scatter.6.cloned.1.call-start = ((), (), s32[]{:S(2)}) async-start(), calls=%async_computation.4 | async-start | bytes 2359296 | tf_op jit(solution)/shard_map/reduce_scatter | solution.py:81
  84.2 7.5 collective-permute-start.3
  92.0 46.9 %collective-permute-start.4 = (f32[2048,256]{0,1:T(8,128)S(1)}, f32[2048,256]{0,1:T(8,128)S(1)}, u32[]{:S(2)}, u32[]{:S(2)}) collective-permute-start(f32[2048,256]{0,1:T(8,128)S(1)} %add.75), channel_id=1, source_target_pairs={{0,2},{1,3},{2,0},{3,1},{4,6},{5,7},{6,4},{7,5},{8,10},{9,11},{10,... | collective-permute-start | bytes 6291464 | tf_op jit(solution)/shard_map/ppermute | solution.py:14
  139.2 47.7 %collective-permute-start.5 = (f32[2048,256]{0,1:T(8,128)S(1)}, f32[2048,256]{0,1:T(8,128)S(1)}, u32[]{:S(2)}, u32[]{:S(2)}) collective-permute-start(f32[2048,256]{0,1:T(8,128)S(1)} %add.76), channel_id=1, source_target_pairs={{0,4},{1,5},{2,6},{3,7},{4,0},{5,1},{6,2},{7,3},{8,12},{9,13},{10,... | collective-permute-start | bytes 6291464 | tf_op jit(solution)/shard_map/ppermute | solution.py:14
  186.9 3.4 copy-start.10
  186.9 3.4 copy-start.19
  192.1 8.4 copy-start.14
  192.1 7.9 copy-start.16
  192.1 7.8 collective-permute-start.6
  193.8 6.7 copy-start.25
  270.6 18.5 %copy-start.4 = (f32[1,4,256,256]{3,2,1,0:T(8,128)}, f32[1,4,256,256]{3,2,1,0:T(8,128)S(1)}, u32[]{:S(2)}) copy-start(f32[1,4,256,256]{3,2,1,0:T(8,128)S(1)} %multiply_subtract_fusion.2) | copy-start | bytes 3145732
  270.6 7.4 collective-permute-start.7
  280.0 9.1 copy-start.11
  280.0 9.0 collective-permute-start.8
  281.4 7.7 copy-start.27
  359.5 7.2 collective-permute-start.9
  373.3 355.7 %reduce-scatter.8.cloned.1.call-start = ((), (), s32[]{:S(2)}) async-start(), calls=%async_computation.5 | async-start | bytes 2359296 | tf_op jit(solution)/shard_map/reduce_scatter | solution.py:81
  408.8 7.5 collective-permute-start.10
  416.6 46.9 %collective-permute-start.11 = (f32[2048,256]{0,1:T(8,128)S(1)}, f32[2048,256]{0,1:T(8,128)S(1)}, u32[]{:S(2)}, u32[]{:S(2)}) collective-permute-start(f32[2048,256]{0,1:T(8,128)S(1)} %add.81), channel_id=1, source_target_pairs={{0,2},{1,3},{2,0},{3,1},{4,6},{5,7},{6,4},{7,5},{8,10},{9,11},{10,... | collective-permute-start | bytes 6291464 | tf_op jit(solution)/shard_map/ppermute | solution.py:14
  463.8 47.9 %collective-permute-start.12 = (f32[2048,256]{0,1:T(8,128)S(1)}, f32[2048,256]{0,1:T(8,128)S(1)}, u32[]{:S(2)}, u32[]{:S(2)}) collective-permute-start(f32[2048,256]{0,1:T(8,128)S(1)} %add.82), channel_id=1, source_target_pairs={{0,4},{1,5},{2,6},{3,7},{4,0},{5,1},{6,2},{7,3},{8,12},{9,13},{10,... | collective-permute-start | bytes 6291464 | tf_op jit(solution)/shard_map/ppermute | solution.py:14
  511.7 3.3 copy-start.21
  516.9 7.6 copy-start.15
  517.0 7.6 collective-permute-start.13
  518.3 6.2 copy-start.26
  595.5 18.5 %copy-start.3 = (f32[1,4,256,256]{3,2,1,0:T(8,128)}, f32[1,4,256,256]{3,2,1,0:T(8,128)S(1)}, u32[]{:S(2)}) copy-start(f32[1,4,256,256]{3,2,1,0:T(8,128)S(1)} %multiply_subtract_fusion.1) | copy-start | bytes 3145732
  595.6 7.5 collective-permute-start.14
  605.0 9.1 copy-start.12
  605.0 9.1 collective-permute-start.15
  606.4 7.7 copy-start.28
  684.1 7.3 copy-start.1
  684.1 7.1 collective-permute-start.16
  732.6 7.5 collective-permute-start.17
  740.4 46.9 %collective-permute-start.18 = (f32[2048,256]{0,1:T(8,128)S(1)}, f32[2048,256]{0,1:T(8,128)S(1)}, u32[]{:S(2)}, u32[]{:S(2)}) collective-permute-start(f32[2048,256]{0,1:T(8,128)S(1)} %add.88), channel_id=1, source_target_pairs={{0,2},{1,3},{2,0},{3,1},{4,6},{5,7},{6,4},{7,5},{8,10},{9,11},{10,... | collective-permute-start | bytes 6291464 | tf_op jit(solution)/shard_map/ppermute | solution.py:14
  787.7 47.5 %collective-permute-start.19 = (f32[2048,256]{0,1:T(8,128)S(1)}, f32[2048,256]{0,1:T(8,128)S(1)}, u32[]{:S(2)}, u32[]{:S(2)}) collective-permute-start(f32[2048,256]{0,1:T(8,128)S(1)} %add.89), channel_id=1, source_target_pairs={{0,4},{1,5},{2,6},{3,7},{4,0},{5,1},{6,2},{7,3},{8,12},{9,13},{10,... | collective-permute-start | bytes 6291464 | tf_op jit(solution)/shard_map/ppermute | solution.py:14
  835.2 3.3 copy-start.7
  840.4 7.6 copy-start.13
  840.4 7.6 collective-permute-start.20
  841.8 6.2 copy-start.24
  (10 other events, 13.3 us)
Sparse Core Ops, SparseCore 0:
  42.1 38.4 reduce-scatter.3
  373.4 31.7 reduce-scatter.5
  697.1 31.8 reduce-scatter.7
